TPU v7x, 32 devices: a whole 2x2x4 slice. The times are simulated.
32 devices in a mesh: grp: 2 (over y), seq: 4 (over z), dp: 2 (over x), pipe: 2 (over core).
Axes of the slice: x: 2, y: 2, z: 4, core: 2. Of those that a mesh axis runs over, the one named last changes fastest.
Arguments:
- embeddings: bfloat16 [4, 512, 1664], P(('grp', 'dp'), 'seq'), parts along dimension 0, may hold values from -650 to 650
- upstream: bfloat16 [4, 512, 1664], P(('grp', 'dp'), 'seq'), parts along dimension 0, may hold values from -6 to 6
- attn_weights: bfloat16 [4, 1664, 832], P(None, ('seq', 'dp'), 'pipe'), may hold values from -1.2747549 to 1.2747549
Outputs:
- input_grads: bfloat16 [4, 512, 1664], P(('grp', 'dp'), 'seq'), parts along dimension 0
- weight_grads: float32 [8, 1664, 832], P('grp', ('seq', 'dp'), 'pipe'), parts along dimension 0
There are 2 independent parts, one for each index of `grp`. A program takes and returns all parts, laid end to end along the dimension named above; an argument that names none is the same for every part. Nothing has to cross between parts.
All inputs are finite; a program needn't handle non-finite values.
Results may differ from a plain program's by a relative error of at most 0.014.
The roundings to bfloat16 on the way count: a program that leaves them out, or rounds other values in their place, can miss the bound.
Values may be sent and summed in bfloat16 or wider, within the bound.
No kernel may reach another device: no remote copies, remote signals or barrier semaphores. Data moves between devices by JAX's collectives and lax.ppermute only.
A program may use at most 128 MiB of HBM per device.

v0:
```python
import math
import jax
import jax.numpy as jnp
from jax import lax
from jax.sharding import PartitionSpec as P

HD = 104
EPSILON = 1e-06


def local(embeddings, upstream, attn_weights):
    tokens = embeddings[0]
    row_gradients = upstream[0]
    row_count = tokens.shape[0]
    weights = lax.all_gather(attn_weights, ("seq", "dp"), axis=1, tiled=True)
    local_width = weights.shape[2]
    head_count = local_width // HD
    score_scale = HD ** (-0.5)
    features = tokens.astype(jnp.float32)
    row_mean = jnp.mean(features, axis=1, keepdims=True)
    mean_removed = features - row_mean
    variance = jnp.mean(mean_removed * mean_removed, axis=1, keepdims=True)
    inverse_deviation = lax.rsqrt(variance + EPSILON)
    standardized_input = mean_removed * inverse_deviation
    normalized_rows = standardized_input.astype(jnp.bfloat16)
    proj = jnp.einsum(
        "td,cdh->cth", normalized_rows, weights[:3], preferred_element_type=jnp.float32
    ).astype(jnp.bfloat16)
    gathered = lax.all_gather(proj[1:], "seq", axis=1, tiled=True)
    key_count = gathered.shape[1]
    query_heads = proj[0].reshape(row_count, head_count, HD).transpose(1, 0, 2)
    key_heads = gathered[0].reshape(key_count, head_count, HD).transpose(1, 0, 2)
    value_heads = gathered[1].reshape(key_count, head_count, HD).transpose(1, 0, 2)
    grad_att = jnp.dot(row_gradients, weights[3], preferred_element_type=jnp.float32).astype(
        jnp.bfloat16
    )
    grad_heads = grad_att.reshape(row_count, head_count, HD).transpose(1, 0, 2)

    def one_head(items):
        query_rows, key_rows, value_rows, grad_out = items
        scores = jnp.dot(query_rows, key_rows.T, preferred_element_type=jnp.float32) * score_scale
        row_max = jnp.max(scores, axis=1, keepdims=True)
        log_total = row_max + jnp.log(jnp.sum(jnp.exp(scores - row_max), axis=1, keepdims=True))
        probs = jnp.exp(scores - log_total).astype(jnp.bfloat16)
        attended = jnp.dot(probs, value_rows, preferred_element_type=jnp.float32).astype(
            jnp.bfloat16
        )
        row_delta = jnp.sum(
            grad_out.astype(jnp.float32) * attended.astype(jnp.float32), axis=1, keepdims=True
        )
        dprobs = jnp.dot(grad_out, value_rows.T, preferred_element_type=jnp.float32)
        dscores = (probs.astype(jnp.float32) * (dprobs - row_delta) * score_scale).astype(
            jnp.bfloat16
        )
        grad_q = jnp.dot(dscores, key_rows, preferred_element_type=jnp.float32).astype(jnp.bfloat16)
        key_term = jnp.dot(dscores.T, query_rows, preferred_element_type=jnp.float32)
        value_term = jnp.dot(probs.T, grad_out, preferred_element_type=jnp.float32)
        return (attended, grad_q, key_term, value_term)

    attended_h, grad_q_h, key_h, value_h = lax.map(
        one_head, (query_heads, key_heads, value_heads, grad_heads)
    )
    attended_flat = attended_h.transpose(1, 0, 2).reshape(row_count, local_width)
    grad_q = grad_q_h.transpose(1, 0, 2).reshape(1, row_count, local_width)
    key_terms = key_h.transpose(1, 0, 2).reshape(key_count, local_width)
    value_terms = value_h.transpose(1, 0, 2).reshape(key_count, local_width)
    both_terms = jnp.stack([key_terms, value_terms])
    owned = lax.psum_scatter(
        both_terms.astype(jnp.bfloat16), "seq", scatter_dimension=1, tiled=True
    )
    grad_qkv = jnp.concatenate([grad_q, owned], axis=0)
    token_count = row_count * lax.axis_size("seq") * lax.axis_size("dp")
    grad_factor = 1.0 / math.sqrt(token_count)
    terms_qkv = jnp.einsum(
        "td,cth->cdh", normalized_rows, grad_qkv, preferred_element_type=jnp.float32
    )
    term_out = jnp.einsum(
        "td,th->dh", row_gradients, attended_flat, preferred_element_type=jnp.float32
    )
    terms = jnp.concatenate([terms_qkv, term_out[None]], axis=0) * grad_factor
    seq_summed = lax.psum_scatter(
        terms.astype(jnp.bfloat16), "seq", scatter_dimension=1, tiled=True
    )
    weight_grads = lax.psum_scatter(seq_summed, "dp", scatter_dimension=1, tiled=True).astype(
        jnp.float32
    )
    input_part = jnp.einsum(
        "cth,cdh->td", grad_qkv, weights[:3], preferred_element_type=jnp.float32
    )
    reduced_total = lax.psum(input_part.astype(jnp.bfloat16), "pipe").astype(jnp.float32)
    leading_term = jnp.mean(reduced_total, axis=1, keepdims=True)
    trailing_term = jnp.mean(reduced_total * standardized_input, axis=1, keepdims=True)
    input_gradient = (
        row_gradients.astype(jnp.float32)
        + inverse_deviation * (reduced_total - leading_term - standardized_input * trailing_term)
    ).astype(jnp.bfloat16)
    return (input_gradient[None], weight_grads)


def solution(mesh):
    in_specs = (
        P(("grp", "dp"), "seq", None),
        P(("grp", "dp"), "seq", None),
        P(None, ("seq", "dp"), "pipe"),
    )
    out_specs = (P(("grp", "dp"), "seq", None), P("grp", ("seq", "dp"), "pipe"))
    return jax.shard_map(local, mesh=mesh, in_specs=in_specs, out_specs=out_specs, check_vma=False)
```

profile of v0, /device:TPU:0, one launch (start us, length us, event | category | flops | bytes accessed | tf_op | source)
XLA Modules:
  0.0 409.7 jit_solution(12918442514962170128)
XLA Ops:
  7.2 2.7 copy.16
  10.0 1.1 convert_reduce_fusion.1
  11.2 1.3 fusion.46
  12.5 106.6 %all-gather.2.cloned.1.call-done = bf16[4,1664,416]{2,0,1:T(4,128)(2,1)} async-done(((bf16[4,208,416]{2,0,1:T(4,128)(2,1)}), bf16[4,1664,416]{2,0,1:T(4,128)(2,1)}) %all-gather.2.cloned.1.call-update) | async-done | bytes 5537808 | tf_op jit(solution)/shard_map/all_gather | solution.py:15
  119.0 11.3 %copy.29 = bf16[3,1664,416]{1,2,0:T(8,128)(2,1)} copy(bf16[3,1664,416]{2,0,1:T(4,128)(2,1)} %bitcast.176) | data formatting | bytes 8306688
  130.3 3.5 fusion.33
  133.8 0.7 slice.27
  134.5 8.4 %slice.30 = bf16[1,1664,416]{2,0,1:T(2,128)(2,1)} slice(bf16[4,1664,416]{2,0,1:T(4,128)(2,1)} %all-gather.2.cloned.1.call-done), slice={[3:4], [0:1664], [0:416]} | slice | bytes 2768896 | tf_op jit(solution)/shard_map/slice | solution.py:34
  142.9 8.5 %copy.30 = bf16[1,1664,416]{1,2,0:T(8,128)(2,1)S(1)} copy(bf16[1,1664,416]{2,0,1:T(2,128)(2,1)} %slice.30) | data formatting | bytes 2768896
  151.5 18.4 %all_gather.7 = bf16[2,512,416]{1,2,0:T(8,128)(2,1)S(1)} all-gather(bf16[2,128,416]{1,2,0:T(8,128)(2,1)} %slice.27), channel_id=1, replica_groups=mesh['grp'=2,'seq'=4,'dp'=2,'pipe'=2] {'seq'}, dimensions={1}, use_global_device_ids=true | all-gather | bytes 1064960 | tf_op jit(solution)/shard_map/all_gather | solution.py:29
  169.9 1.0 fusion.57
  170.9 1.3 copy.19
  172.2 1.3 copy.20
  173.5 0.5 fusion.34
  174.0 16.9 %while.16 = (s32[]{:T(128)}, bf16[4,128,104]{1,2,0:T(8,128)(2,1)}, bf16[4,128,104]{1,2,0:T(8,128)(2,1)}, bf16[4,512,104]{1,2,0:T(8,128)(2,1)}, bf16[4,512,104]{1...) while((s32[]{:T(128)}, bf16[4,128,104]{1,2,0:T(8,128)(2,1)}, ...), condition=%wide.region_6.7_spmd, body=%wide.region_2.6_spmd.sunk | while | flops 82589440 | bytes 2916977 | solution.py:60
  174.0 0.3 fusion.88
  174.3 0.2 exponential_reduce_fusion.2
  174.7 0.8 bitcast_dynamic-update-slice_fusion.2
  175.5 0.2 fusion.89
  175.8 0.9 fusion.90
  176.6 0.9 fusion.91
  177.5 0.8 fusion.92
  178.3 0.3 fusion.88
  178.6 0.2 exponential_reduce_fusion.2
  178.9 0.8 bitcast_dynamic-update-slice_fusion.2
  179.8 0.2 fusion.89
  180.0 0.8 fusion.90
  180.9 0.9 fusion.91
  181.7 0.8 fusion.92
  182.5 0.3 fusion.88
  182.8 0.2 exponential_reduce_fusion.2
  183.1 0.8 bitcast_dynamic-update-slice_fusion.2
  184.0 0.2 fusion.89
  184.2 0.8 fusion.90
  185.1 0.9 fusion.91
  185.9 0.8 fusion.92
  186.7 0.3 fusion.88
  187.0 0.2 exponential_reduce_fusion.2
  187.4 0.8 bitcast_dynamic-update-slice_fusion.2
  188.2 0.2 fusion.89
  188.5 0.8 fusion.90
  189.3 0.9 fusion.91
  190.2 0.8 fusion.92
  191.0 1.2 pad_maximum_fusion
  192.2 1.0 copy.23
  193.2 1.7 reshape.49
  195.0 1.5 convolution_bitcast_fusion.3
  196.5 21.9 %reduce-scatter.10.cloned.1.call-done = bf16[128,832]{1,0:T(8,128)(2,1)} async-done(((bf16[512,832]{1,0:T(8,128)(2,1)}), bf16[128,832]{1,0:T(8,128)(2,1)}) %reduce-scatter.10.cloned.1.call-update) | async-done | bytes 213008
  218.5 1.9 reshape.50
  220.4 1.1 copy.24
  221.5 1.3 convolution_bitcast_fusion.2
  222.9 3.3 fusion.29
  226.1 11.9 %copy.25 = bf16[4,1664,416]{2,0,1:T(4,128)(2,1)} copy(bf16[4,1664,416]{1,2,0:T(8,128)(2,1)} %fusion.29) | data formatting | bytes 11075584
  238.1 12.9 %reshape.51 = bf16[1664,1664]{1,0:T(8,128)(2,1)} reshape(bf16[1664,4,416]{2,1,0:T(4,128)(2,1)} %bitcast.175) | data formatting | bytes 11075584
  251.0 3.8 fusion.30
  254.8 0.2 reduce-scatter.14.cloned.1.call-start
  255.1 93.5 %reduce-scatter.12.cloned.1.call-done = bf16[416,1664]{1,0:T(8,128)(2,1)} async-done(((bf16[1664,1664]{1,0:T(8,128)(2,1)}), bf16[416,1664]{1,0:T(8,128)(2,1)}) %reduce-scatter.12.cloned.1.call-update) | async-done | bytes 1384464
  348.6 21.9 %all-reduce.2.cloned.1.call-done = bf16[128,1664]{1,0:T(8,128)(2,1)} async-done(((bf16[128,1664]{1,0:T(8,128)(2,1)}), bf16[128,1664]{1,0:T(8,128)(2,1)}) %all-reduce.2.cloned.1.call-update) | async-done | bytes 426000 | tf_op jit(solution)/shard_map/psum | solution.py:90
  370.5 1.3 convert_reduce_fusion
  371.8 2.2 fusion.48
  374.0 23.8 %reduce-scatter.14.cloned.1.call-done = bf16[208,1664]{1,0:T(8,128)(2,1)} async-done(((bf16[416,1664]{1,0:T(8,128)(2,1)}), bf16[208,1664]{1,0:T(8,128)(2,1)}) %reduce-scatter.14.cloned.1.call-update) | async-done | bytes 692240
  397.8 3.1 reshape.54
  400.9 0.8 copy.28
  401.7 1.5 copy.22
  (40 shorter events, 1.1 us)
Async XLA Ops:
  7.2 111.9 %all-gather.2.cloned.1.call-start = ((), (), s32[]{:S(2)}) async-start(), calls=%async_computation.3 | async-start | bytes 7667712 | tf_op jit(solution)/shard_map/all_gather | solution.py:15
  10.0 208.5 %reduce-scatter.10.cloned.1.call-start = ((), (), s32[]{:S(2)}) async-start(), calls=%async_computation.5 | async-start | bytes 1146880
  119.0 11.3 %copy-start = (bf16[1,128,1664]{2,1,0:T(8,128)(2,1)S(1)}, bf16[1,128,1664]{2,1,0:T(8,128)(2,1)}, u32[]{:S(2)}) copy-start(bf16[1,128,1664]{2,1,0:T(8,128)(2,1)} %param.5) | copy-start | bytes 1277956
  142.9 30.6 %copy-start.1 = (bf16[1,128,1664]{2,1,0:T(8,128)(2,1)S(1)}, bf16[1,128,1664]{2,1,0:T(8,128)(2,1)}, u32[]{:S(2)}) copy-start(bf16[1,128,1664]{2,1,0:T(8,128)(2,1)} %param.6) | copy-start | bytes 1277956
  191.0 4.0 copy-start.4
  192.2 29.3 %copy-start.3 = (bf16[4,128,104]{1,2,0:T(8,128)(2,1)S(1)}, bf16[4,128,104]{1,2,0:T(8,128)(2,1)}, u32[]{:S(2)}) copy-start(bf16[4,128,104]{1,2,0:T(8,128)(2,1)} %get-tuple-element.52) | copy-start | bytes 319492
  195.0 153.6 %reduce-scatter.12.cloned.1.call-start = ((), (), s32[]{:S(2)}) async-start(), calls=%async_computation.6 | async-start | bytes 6922240
  251.0 120.9 %copy-start.2 = (bf16[1,128,1664]{2,1,0:T(8,128)(2,1)S(1)}, bf16[1,128,1664]{2,1,0:T(8,128)(2,1)}, u32[]{:S(2)}) copy-start(bf16[1,128,1664]{2,1,0:T(8,128)(2,1)} %param.6) | copy-start | bytes 1277956
  251.0 119.5 %all-reduce.2.cloned.1.call-start = ((), (), s32[]{:S(2)}) async-start(), calls=%async_computation.4 | async-start | bytes 851968 | tf_op jit(solution)/shard_map/psum | solution.py:90
  254.8 143.0 %reduce-scatter.14.cloned.1.call-start = ((), (), s32[]{:S(2)}) async-start(), calls=%async_computation.7 | async-start | bytes 2076672
Sparse Core Ops, SparseCore 0:
  10.8 108.2 all-gather.1
  195.1 23.3 reduce-scatter.9
  251.1 97.4 reduce-scatter.11
  351.4 19.0 all-reduce.1
  372.6 25.1 reduce-scatter.13
where the time goes:
time: 411 us; the launch traced here: 410 us
  waiting for transfers between devices  268 us (65%)
  local copies, waits for them, and re-layouts  71.1 us (17%)
  matrix products  26 us (6%)
  blocking collectives  18.4 us (4%)
  between operations  13.9 us (3%)
  other arithmetic  11.9 us (3%)
    unnamed x8, waiting for transfers between devices  139 us
    all_gather x1, waiting for transfers between devices, local(): weights = lax.all_gather(attn_weights, ('seq', 'dp'), axis=1, tiled=True)  107 us
    unnamed x22, local copies, waits for them, and re-layouts  58.4 us
    psum x1, waiting for transfers between devices, local(): lax.psum(input_part.astype(jnp.bfloat16), 'pipe').astype(jnp.float32)  21.9 us
    all_gather x1, blocking collectives, local(): gathered = lax.all_gather(proj[1:], 'seq', axis=1, tiled=True)  18.4 us
    slice x1, local copies, waits for them, and re-layouts, local(): weights[3]  8.39 us
  transfers between devices with their start and end apart: 5, of which 5 were waited for; matrix products, arithmetic and copies ran while one was open for 3% of the time, Pallas kernels for 0%

commit v1 on v0

--- a/solution.py
+++ b/solution.py
@@ -87,7 +87,9 @@
     input_part = jnp.einsum(
         "cth,cdh->td", grad_qkv, weights[:3], preferred_element_type=jnp.float32
     )
-    reduced_total = lax.psum(input_part.astype(jnp.bfloat16), "pipe").astype(jnp.float32)
+    reduced_total = jnp.sum(lax.all_gather(input_part.astype(jnp.bfloat16), "pipe"), axis=0).astype(
+        jnp.float32
+    )
     leading_term = jnp.mean(reduced_total, axis=1, keepdims=True)
     trailing_term = jnp.mean(reduced_total * standardized_input, axis=1, keepdims=True)
     input_gradient = (

time: 411 us -> 389 us (0.946)
  waiting for transfers between devices: 268 us -> 245 us
    psum x1 -> x0, waiting for transfers between devices: 21.9 us -> none  [local(): lax.psum(input_part.astype(jnp.bfloat16), 'pipe').astype(jnp.float32)]
    unnamed x8 -> x7, waiting for transfers between devices: 139 us -> 139 us
  transfers between devices with their start and end apart: 5 -> 4, of which waited for: 5 -> 4; matrix products, arithmetic and copies ran while one was open for 3% -> 2% of each run, Pallas kernels for 0% -> 0%
where the time goes in v1:
time: 389 us; the launch traced here: 387 us
  waiting for transfers between devices  245 us (63%)
  local copies, waits for them, and re-layouts  71.1 us (18%)
  matrix products  25.3 us (7%)
  blocking collectives  21 us (5%)
  between operations  13.9 us (4%)
  other arithmetic  10.2 us (3%)
    unnamed x7, waiting for transfers between devices  139 us
    all_gather x1, waiting for transfers between devices, local(): weights = lax.all_gather(attn_weights, ('seq', 'dp'), axis=1, tiled=True)  107 us
    unnamed x22, local copies, waits for them, and re-layouts  58.4 us
    all_gather x1, blocking collectives, local(): gathered = lax.all_gather(proj[1:], 'seq', axis=1, tiled=True)  18.4 us
    slice x1, local copies, waits for them, and re-layouts, local(): weights[3]  8.39 us
  transfers between devices with their start and end apart: 4, of which 4 were waited for; matrix products, arithmetic and copies ran while one was open for 2% of the time, Pallas kernels for 0%

profile of v1, /device:TPU:0, one launch (start us, length us, event | category | flops | bytes accessed | tf_op | source)
XLA Modules:
  0.0 387.2 jit_solution(7931240560010690095)
XLA Ops:
  7.2 2.7 copy.16
  10.0 1.1 convert_reduce_fusion.1
  11.2 1.3 fusion.41
  12.5 106.6 %all-gather.3.cloned.1.call-done = bf16[4,1664,416]{2,0,1:T(4,128)(2,1)} async-done(((bf16[4,208,416]{2,0,1:T(4,128)(2,1)}), bf16[4,1664,416]{2,0,1:T(4,128)(2,1)}) %all-gather.3.cloned.1.call-update) | async-done | bytes 5537808 | tf_op jit(solution)/shard_map/all_gather | solution.py:15
  119.0 11.3 %copy.29 = bf16[3,1664,416]{1,2,0:T(8,128)(2,1)} copy(bf16[3,1664,416]{2,0,1:T(4,128)(2,1)} %bitcast.168) | data formatting | bytes 8306688
  130.3 3.5 fusion.33
  133.8 0.7 slice.27
  134.5 8.4 %slice.30 = bf16[1,1664,416]{2,0,1:T(2,128)(2,1)} slice(bf16[4,1664,416]{2,0,1:T(4,128)(2,1)} %all-gather.3.cloned.1.call-done), slice={[3:4], [0:1664], [0:416]} | slice | bytes 2768896 | tf_op jit(solution)/shard_map/slice | solution.py:34
  142.9 8.5 %copy.30 = bf16[1,1664,416]{1,2,0:T(8,128)(2,1)S(1)} copy(bf16[1,1664,416]{2,0,1:T(2,128)(2,1)} %slice.30) | data formatting | bytes 2768896
  151.5 18.4 %all_gather.13 = bf16[2,512,416]{1,2,0:T(8,128)(2,1)S(1)} all-gather(bf16[2,128,416]{1,2,0:T(8,128)(2,1)} %slice.27), channel_id=1, replica_groups=mesh['grp'=2,'seq'=4,'dp'=2,'pipe'=2] {'seq'}, dimensions={1}, use_global_device_ids=true | all-gather | bytes 1064960 | tf_op jit(solution)/shard_map/all_gather | solution.py:29
  169.9 1.0 fusion.58
  170.9 1.3 copy.19
  172.2 1.3 copy.20
  173.5 0.5 fusion.34
  174.0 16.9 %while.16 = (s32[]{:T(128)}, bf16[4,128,104]{1,2,0:T(8,128)(2,1)}, bf16[4,128,104]{1,2,0:T(8,128)(2,1)}, bf16[4,512,104]{1,2,0:T(8,128)(2,1)}, bf16[4,512,104]{1...) while((s32[]{:T(128)}, bf16[4,128,104]{1,2,0:T(8,128)(2,1)}, ...), condition=%wide.region_6.7_spmd, body=%wide.region_2.6_spmd.sunk | while | flops 82589440 | bytes 2916977 | solution.py:60
  174.0 0.3 fusion.89
  174.3 0.2 exponential_reduce_fusion.2
  174.7 0.8 bitcast_dynamic-update-slice_fusion.2
  175.5 0.2 fusion.90
  175.8 0.9 fusion.91
  176.6 0.9 fusion.92
  177.5 0.8 fusion.93
  178.3 0.3 fusion.89
  178.6 0.2 exponential_reduce_fusion.2
  178.9 0.8 bitcast_dynamic-update-slice_fusion.2
  179.8 0.2 fusion.90
  180.0 0.8 fusion.91
  180.9 0.9 fusion.92
  181.7 0.8 fusion.93
  182.5 0.3 fusion.89
  182.8 0.2 exponential_reduce_fusion.2
  183.1 0.8 bitcast_dynamic-update-slice_fusion.2
  184.0 0.2 fusion.90
  184.2 0.8 fusion.91
  185.1 0.9 fusion.92
  185.9 0.8 fusion.93
  186.7 0.3 fusion.89
  187.0 0.2 exponential_reduce_fusion.2
  187.4 0.8 bitcast_dynamic-update-slice_fusion.2
  188.2 0.2 fusion.90
  188.5 0.8 fusion.91
  189.3 0.9 fusion.92
  190.2 0.8 fusion.93
  191.0 1.2 pad_maximum_fusion
  192.2 1.0 copy.23
  193.2 1.7 reshape.110
  195.0 1.5 convolution_bitcast_fusion.3
  196.5 21.9 %reduce-scatter.10.cloned.1.call-done = bf16[128,832]{1,0:T(8,128)(2,1)} async-done(((bf16[512,832]{1,0:T(8,128)(2,1)}), bf16[128,832]{1,0:T(8,128)(2,1)}) %reduce-scatter.10.cloned.1.call-update) | async-done | bytes 213008
  218.5 1.9 reshape.111
  220.4 1.1 copy.24
  221.5 1.3 convolution_bitcast_fusion.2
  222.9 3.3 fusion.29
  226.1 11.9 %copy.25 = bf16[4,1664,416]{2,0,1:T(4,128)(2,1)} copy(bf16[4,1664,416]{1,2,0:T(8,128)(2,1)} %fusion.29) | data formatting | bytes 11075584
  238.1 12.9 %reshape.112 = bf16[1664,1664]{1,0:T(8,128)(2,1)} reshape(bf16[1664,4,416]{2,1,0:T(4,128)(2,1)} %bitcast.167) | data formatting | bytes 11075584
  251.0 97.6 %reduce-scatter.12.cloned.1.call-done = bf16[416,1664]{1,0:T(8,128)(2,1)} async-done(((bf16[1664,1664]{1,0:T(8,128)(2,1)}), bf16[416,1664]{1,0:T(8,128)(2,1)}) %reduce-scatter.12.cloned.1.call-update) | async-done | bytes 1384464
  348.6 3.0 fusion.30
  351.6 2.6 all-gather
  354.2 0.3 reduce_sum.68
  354.5 0.3 convert_reduce_fusion
  354.9 1.2 fusion.47
  356.1 19.2 %reduce-scatter.14.cloned.1.call-done = bf16[208,1664]{1,0:T(8,128)(2,1)} async-done(((bf16[416,1664]{1,0:T(8,128)(2,1)}), bf16[208,1664]{1,0:T(8,128)(2,1)}) %reduce-scatter.14.cloned.1.call-update) | async-done | bytes 692240
  375.3 3.1 reshape.115
  378.4 0.8 copy.28
  379.2 1.5 copy.22
  (39 shorter events, 1.1 us)
Async XLA Ops:
  7.2 111.9 %all-gather.3.cloned.1.call-start = ((), (), s32[]{:S(2)}) async-start(), calls=%async_computation.3 | async-start | bytes 7667712 | tf_op jit(solution)/shard_map/all_gather | solution.py:15
  10.0 208.5 %reduce-scatter.10.cloned.1.call-start = ((), (), s32[]{:S(2)}) async-start(), calls=%async_computation.4 | async-start | bytes 1146880
  119.0 11.3 %copy-start = (bf16[1,128,1664]{2,1,0:T(8,128)(2,1)S(1)}, bf16[1,128,1664]{2,1,0:T(8,128)(2,1)}, u32[]{:S(2)}) copy-start(bf16[1,128,1664]{2,1,0:T(8,128)(2,1)} %param.5) | copy-start | bytes 1277956
  142.9 30.6 %copy-start.1 = (bf16[1,128,1664]{2,1,0:T(8,128)(2,1)S(1)}, bf16[1,128,1664]{2,1,0:T(8,128)(2,1)}, u32[]{:S(2)}) copy-start(bf16[1,128,1664]{2,1,0:T(8,128)(2,1)} %param.6) | copy-start | bytes 1277956
  191.0 4.0 %copy-start.4 = (bf16[4,128,104]{1,2,0:T(8,128)(2,1)S(1)}, bf16[4,128,104]{1,2,0:T(8,128)(2,1)}, u32[]{:S(2)}) copy-start(bf16[4,128,104]{1,2,0:T(8,128)(2,1)} %get-tuple-element.55) | copy-start | bytes 319492
  192.2 29.3 %copy-start.3 = (bf16[4,128,104]{1,2,0:T(8,128)(2,1)S(1)}, bf16[4,128,104]{1,2,0:T(8,128)(2,1)}, u32[]{:S(2)}) copy-start(bf16[4,128,104]{1,2,0:T(8,128)(2,1)} %get-tuple-element.52) | copy-start | bytes 319492
  195.0 153.6 %reduce-scatter.12.cloned.1.call-start = ((), (), s32[]{:S(2)}) async-start(), calls=%async_computation.5 | async-start | bytes 6922240
  251.0 124.3 %reduce-scatter.14.cloned.1.call-start = ((), (), s32[]{:S(2)}) async-start(), calls=%async_computation.6 | async-start | bytes 2076672
  348.6 6.3 %copy-start.2 = (bf16[1,128,1664]{2,1,0:T(8,128)(2,1)S(1)}, bf16[1,128,1664]{2,1,0:T(8,128)(2,1)}, u32[]{:S(2)}) copy-start(bf16[1,128,1664]{2,1,0:T(8,128)(2,1)} %param.6) | copy-start | bytes 1277956
Sparse Core Ops, SparseCore 0:
  10.8 108.2 all-gather.2
  195.1 23.3 reduce-scatter.9
  251.1 97.4 reduce-scatter.11
  350.7 24.5 reduce-scatter.13
